TPU v7x, 32 devices: a whole 2x2x4 slice. The times are simulated.
32 devices in a mesh: pair: 8 (over z, x), occ: 4 (over y, core).
Axes of the slice: x: 2, y: 2, z: 4, core: 2. Of those that a mesh axis runs over, the one named last changes fastest.
Arguments:
- integrals: bfloat16 [8, 64, 64, 1024], P('pair', None, None, 'occ'), may hold values from -6 to 6
- occ_coeffs: bfloat16 [6144, 128], replicated, may hold values from -0.125 to 0.125
- virt_coeffs: bfloat16 [6144, 5120], P(None, 'pair'), may hold values from -0.078125 to 0.078125
- block_ids: int32 [2, 8, 64], P(None, 'pair'), may hold values from 0 to 95, as said below
- live_mask: int32 [8, 64], P('pair'), may hold values from 0 to 1, as said below
Outputs:
- factors: bfloat16 [128, 16, 5120], P('occ', None, 'pair')
Inputs may be any that keep to these rules, and one draw needn't show every extreme that they name: `block_ids`: slot s of pair index p holds a nu block N with N // 12 == s // 8; each (mu block, nu block) pair is held by at most one slot of all pair indices. `live_mask`: among the 8 slots s with the same s // 8 of one pair index, at most 4 are 1, and exactly 4 for some such group of every pair index.
All inputs are finite; a program needn't handle non-finite values.
Results may differ from a plain program's by a relative error of at most 0.017.
Values may be sent and summed in bfloat16 or wider, within the bound.
No kernel may reach another device: no remote copies, remote signals or barrier semaphores. Data moves between devices by JAX's collectives and lax.ppermute only.
A program may use at most 64 MiB of HBM per device.

v0:
```python
import jax
import jax.numpy as jnp
from jax import lax
from jax.sharding import PartitionSpec as P

LIVE = 4


def half_transform(block_data, mu_index, coeff_blocks):
    slot_count, block_width = (block_data.shape[0], block_data.shape[1])
    aux_local = block_data.shape[2] // block_width
    coeff_rows = jnp.take(coeff_blocks, mu_index, axis=0)
    shaped = block_data.reshape(slot_count, block_width, aux_local, block_width)
    return jnp.einsum("snqm,smi->snqi", shaped, coeff_rows, preferred_element_type=jnp.float32)


def on_device(integrals, occ_coeffs, virt_coeffs, block_ids, live_mask):
    blocks = integrals[0]
    slot_count, block_width = (blocks.shape[0], blocks.shape[1])
    aux_local = blocks.shape[2] // block_width
    occ_count = occ_coeffs.shape[1]
    block_count = occ_coeffs.shape[0] // block_width
    owners = lax.axis_size("pair")
    owned_count = block_count // owners
    group_size = slot_count // owners
    coeff_blocks = occ_coeffs.reshape(block_count, block_width, occ_count)
    mu_index = block_ids[0, 0]
    nu_index = block_ids[1, 0]
    live_flags = live_mask[0]
    grouped_live = live_flags.reshape(owners, group_size)
    sort_keys = (1 - grouped_live) * group_size + jnp.arange(group_size)[None, :]
    chosen = jnp.argsort(sort_keys, axis=1)[:, :LIVE]
    valid_flags = jnp.take_along_axis(grouped_live, chosen, axis=1).reshape(-1)
    slot_index = (chosen + jnp.arange(owners)[:, None] * group_size).reshape(-1)
    send_blocks = blocks[slot_index] * valid_flags[:, None, None].astype(jnp.bfloat16)
    send_blocks = send_blocks.reshape(owners, LIVE, block_width, aux_local * block_width)
    send_mu = mu_index[slot_index].reshape(owners, LIVE)
    send_nu = nu_index[slot_index].reshape(owners, LIVE)
    got_blocks, got_mu, got_nu = (
        lax.all_to_all(send_blocks, "pair", split_axis=0, concat_axis=0, tiled=True),
        lax.all_to_all(send_mu, "pair", split_axis=0, concat_axis=0, tiled=True),
        lax.all_to_all(send_nu, "pair", split_axis=0, concat_axis=0, tiled=True),
    )
    partial_terms = half_transform(
        got_blocks.reshape(owners * LIVE, block_width, -1), got_mu.reshape(-1), coeff_blocks
    )
    selector = got_nu.reshape(-1)[None, :] % owned_count == jnp.arange(owned_count)[:, None]
    summed = jnp.dot(
        selector.astype(jnp.float32),
        partial_terms.reshape(owners * LIVE, -1),
        precision=lax.Precision.HIGHEST,
    )
    summed = summed.reshape(owned_count, block_width, aux_local, occ_count)
    half_sums = summed.astype(jnp.bfloat16)
    slab_sums = lax.all_to_all(half_sums, "occ", split_axis=3, concat_axis=2, tiled=True)
    aux_count, slab_rows = (slab_sums.shape[2], slab_sums.shape[3])
    shard_piece = lax.all_gather(slab_sums, "pair", axis=0, tiled=True)
    piece_blocks = shard_piece.shape[0]
    flat_piece = shard_piece.reshape(piece_blocks * block_width, aux_count, slab_rows)
    result = jnp.einsum("nqi,na->iqa", flat_piece, virt_coeffs, preferred_element_type=jnp.float32)
    return result.astype(jnp.bfloat16)


def solution(mesh):
    return jax.shard_map(
        on_device,
        mesh=mesh,
        in_specs=(
            P("pair", None, None, "occ"),
            P(),
            P(None, "pair"),
            P(None, "pair", None),
            P("pair", None),
        ),
        out_specs=P("occ", None, "pair"),
        check_vma=False,
    )
```

profile of v0, /device:TPU:0, one launch (start us, length us, event | category | flops | bytes accessed | tf_op | source)
XLA Modules:
  0.0 337.0 jit_solution(16466119769843120083)
XLA Ops:
  7.9 1.2 reduce.12
  12.5 7.3 %all-to-all-start.2 = ((s32[8,1,4]{2,1,0:T(1,128)}), s32[8,1,4]{2,1,0:T(1,128)S(1)}, u32[]{:S(2)}, u32[]{:S(2)}) async-start(s32[8,1,4]{2,1,0:T(1,128)} %bitcast.9), calls=%async_computation.2 | async-start | bytes 8192 | tf_op jit(solution)/shard_map/all_to_all | solution.py:41
  21.9 4.3 %all-to-all-done.2 = s32[8,1,4]{2,1,0:T(1,128)S(1)} async-done(((s32[8,1,4]{2,1,0:T(1,128)}), s32[8,1,4]{2,1,0:T(1,128)S(1)}, u32[]{:S(2)}, u32[]{:S(2)}) %all-to-all-start.2) | async-done | bytes 160 | tf_op jit(solution)/shard_map/all_to_all | solution.py:41
  26.2 3.3 all-to-all-start
  29.6 1.1 broadcast_multiply_fusion
  30.7 5.3 %all-to-all-done = s32[8,1,4]{2,1,0:T(1,128)S(1)} async-done(((s32[8,1,4]{2,1,0:T(1,128)}), s32[8,1,4]{2,1,0:T(1,128)S(1)}, u32[]{:S(2)}, u32[]{:S(2)}) %all-to-all-start) | async-done | bytes 160 | tf_op jit(solution)/shard_map/all_to_all | solution.py:42
  36.0 3.6 %all-to-all-start.1 = ((bf16[8,4,64,256]{3,2,1,0:T(8,128)(2,1)}), bf16[8,4,64,256]{3,2,1,0:T(8,128)(2,1)S(1)}, u32[]{:S(2)}, u32[]{:S(2)}) async-start(bf16[8,4,64,256]{3,2,1,0:T(8,128)(2,1)} %broadcast_multiply_fusion), calls=%async_computation.1 | async-start | bytes 2097152 | tf_op jit(solution)/shard_map/all_to_all | solution.py:40
  40.5 2.8 gather_fusion.3
  43.3 19.8 %all-to-all-done.1 = bf16[8,4,64,256]{3,2,1,0:T(8,128)(2,1)S(1)} async-done(((bf16[8,4,64,256]{3,2,1,0:T(8,128)(2,1)}), bf16[8,4,64,256]{3,2,1,0:T(8,128)(2,1)S(1)}, u32[]{:S(2)}, u32[]{:S(2)}) %all-to-all-start.1) | async-done | bytes 1048608 | tf_op jit(solution)/shard_map/all_to_all | solution.py:40
  64.0 1.8 fusion.4
  65.8 5.6 %copy.44 = f32[32,64,4,128]{3,2,1,0:T(4,128)} copy(f32[32,64,4,128]{3,1,2,0:T(8,128)S(1)} %fusion.4) | data formatting | bytes 8388608 | tf_op jit(solution)/shard_map/snqm,smi->snqi/dot_general | solution.py:14
  71.3 5.7 %reshape.146 = f32[32,32768]{1,0:T(8,128)} reshape(f32[32,64,4,128]{3,2,1,0:T(4,128)} %copy.44) | data formatting | bytes 8388608 | tf_op jit(solution)/shard_map/reshape | solution.py:50
  77.0 6.0 %dot_general.15 = f32[64,4,128,32]{2,1,0,3:T(4,128)} reshape(f32[32768,32]{0,1:T(8,128)} %bitcast.54) | data formatting | bytes 8388608 | tf_op jit(solution)/shard_map/dot_general | solution.py:48
  83.0 5.9 %fusion.6 = bf16[12,64,4,128]{3,0,2,1:T(8,128)(2,1)S(1)} fusion(f32[64,4,128,32]{2,1,0,3:T(4,128)} %dot_general.15, s32[32]{0:T(128)S(1)} %and_select_fusion), kind=kOutput, calls=%fused_computation.11 | convolution fusion | flops 151388544 | bytes 4980864 | tf_op jit(solution)/shard_map/dot_general | solution.py:48
  88.9 4.1 %copy.46 = bf16[12,64,4,128]{1,2,0,3:T(4,128)(2,1)S(1)} copy(bf16[12,64,4,128]{3,0,2,1:T(8,128)(2,1)S(1)} %fusion.6) | data formatting | bytes 1572864 | tf_op jit(solution)/shard_map/convert_element_type | solution.py:54
  93.0 1.4 reshape.218
  94.4 14.7 %all_to_all.41 = bf16[4,2,49152]{2,1,0:T(2,128)(2,1)} all-to-all(bf16[4,2,49152]{2,1,0:T(2,128)(2,1)S(1)} %reshape.218), channel_id=1, replica_groups=mesh['pair'=8,'occ'=4] {'occ'}, dimensions={0} | all-to-all | bytes 1572864 | tf_op jit(solution)/shard_map/all_to_all | solution.py:55
  109.1 2.8 reshape.219
  112.3 1.6 copy.48
  113.9 174.2 %all-gather.2.cloned.1.call-done = bf16[96,64,16,32]{1,3,2,0:T(8,128)(2,1)} async-done(((bf16[12,64,16,32]{1,3,2,0:T(8,128)(2,1)}), bf16[96,64,16,32]{1,3,2,0:T(8,128)(2,1)}) %all-gather.2.cloned.1.call-update) | async-done | bytes 6291472 | tf_op jit(solution)/shard_map/all_gather | solution.py:57
  288.1 14.5 %copy.49 = bf16[96,64,16,32]{1,0,3,2:T(8,128)(2,1)} copy(bf16[96,64,16,32]{1,3,2,0:T(8,128)(2,1)} %all-gather.2.cloned.1.call-done) | data formatting | bytes 12582912 | tf_op jit(solution)/shard_map/all_gather | solution.py:57
  302.6 16.9 %reshape.147 = bf16[6144,16,32]{0,2,1:T(8,128)(2,1)} reshape(bf16[96,64,16,32]{1,0,3,2:T(8,128)(2,1)} %copy.49) | data formatting | bytes 12582912 | tf_op jit(solution)/shard_map/reshape | solution.py:59
  319.5 9.6 %fusion.12 = bf16[32,16,640]{2,0,1:T(8,128)(2,1)S(1)} fusion(bf16[6144,16,32]{0,2,1:T(8,128)(2,1)} %reshape.147, bf16[6144,640]{1,0:T(8,128)(2,1)} %param.7), kind=kOutput, calls=%fused_computation.13 | convolution fusion | flops 4026859520 | bytes 14811136 | tf_op jit(solution)/shard_map/nqi,na->iqa/dot_general | solution.py:60
  329.1 1.0 copy.50
  (42 shorter events, 9.0 us)
Async XLA Ops:
  6.5 14.7 %copy-start = (bf16[1,64,64,256]{3,2,1,0:T(8,128)(2,1)S(1)}, bf16[1,64,64,256]{3,2,1,0:T(8,128)(2,1)}, u32[]{:S(2)}) copy-start(bf16[1,64,64,256]{3,2,1,0:T(8,128)(2,1)} %param.5) | copy-start | bytes 6291460
  12.5 13.7 %all-to-all-start.2 = ((s32[8,1,4]{2,1,0:T(1,128)}), s32[8,1,4]{2,1,0:T(1,128)S(1)}, u32[]{:S(2)}, u32[]{:S(2)}) async-start(s32[8,1,4]{2,1,0:T(1,128)} %bitcast.9), calls=%async_computation.2 | async-start | bytes 8192 | tf_op jit(solution)/shard_map/all_to_all | solution.py:41
  26.2 9.8 %all-to-all-start = ((s32[8,1,4]{2,1,0:T(1,128)}), s32[8,1,4]{2,1,0:T(1,128)S(1)}, u32[]{:S(2)}, u32[]{:S(2)}) async-start(s32[8,1,4]{2,1,0:T(1,128)} %bitcast.2), calls=%async_computation | async-start | bytes 8192 | tf_op jit(solution)/shard_map/all_to_all | solution.py:42
  36.0 27.1 %all-to-all-start.1 = ((bf16[8,4,64,256]{3,2,1,0:T(8,128)(2,1)}), bf16[8,4,64,256]{3,2,1,0:T(8,128)(2,1)S(1)}, u32[]{:S(2)}, u32[]{:S(2)}) async-start(bf16[8,4,64,256]{3,2,1,0:T(8,128)(2,1)} %broadcast_multiply_fusion), calls=%async_computation.1 | async-start | bytes 2097152 | tf_op jit(solution)/shard_map/all_to_all | solution.py:40
  39.6 248.5 %all-gather.2.cloned.1.call-start = ((), (), s32[]{:S(2)}) async-start(), calls=%async_computation.4 | async-start | bytes 14155776 | tf_op jit(solution)/shard_map/all_gather | solution.py:57
  319.5 10.6 %copy-start.1 = (bf16[1,64,64,256]{3,2,1,0:T(8,128)(2,1)S(1)}, bf16[1,64,64,256]{3,2,1,0:T(8,128)(2,1)}, u32[]{:S(2)}) copy-start(bf16[1,64,64,256]{3,2,1,0:T(8,128)(2,1)} %param.5) | copy-start | bytes 6291460
Sparse Core Ops, SparseCore 0:
  114.1 173.9 all-gather.1
where the time goes:
time: 338 us; the launch traced here: 337 us
  waiting for transfers between devices  204 us (60%)
  local copies, waits for them, and re-layouts  70 us (21%)
  matrix products  17.3 us (5%)
  blocking collectives  14.7 us (4%)
  starting transfers between devices  14.2 us (4%)
  between operations  13.5 us (4%)
  other arithmetic  3.69 us (1%)
    all_gather x1, waiting for transfers between devices, on_device(): shard_piece = lax.all_gather(slab_sums, 'pair', axis=0, tiled=True)  174 us
    all_to_all x1, waiting for transfers between devices, on_device(): lax.all_to_all(send_blocks, 'pair', split_axis=0, concat_axis=0, tiled=True)  19.8 us
    reshape x1, local copies, waits for them, and re-layouts, on_device(): shard_piece.reshape(piece_blocks * block_width, aux_count, slab_rows)  16.9 us
    all_to_all x1, blocking collectives, on_device(): lax.all_to_all(half_sums, 'occ', split_axis=3, concat_axis=2, tiled=True)  14.7 us
    all_gather x1, local copies, waits for them, and re-layouts, on_device(): shard_piece = lax.all_gather(slab_sums, 'pair', axis=0, tiled=True)  14.5 us
    dot_general x1, matrix products, on_device(): jnp.einsum('nqi,na->iqa', flat_piece, virt_coeffs, preferred_element_type...  9.58 us
    all_to_all x1, starting transfers between devices, on_device(): lax.all_to_all(send_mu, 'pair', split_axis=0, concat_axis=0, tiled=True)  7.28 us
  transfers between devices with their start and end apart: 4, of which 4 were waited for; matrix products, arithmetic and copies ran while one was open for 2% of the time, Pallas kernels for 0%

commit v1 on v0

--- a/solution.py
+++ b/solution.py
@@ -4,6 +4,28 @@
 from jax.sharding import PartitionSpec as P
 
 LIVE = 4
+
+
+def laid_out(blocks, dim):
+    blocks = jnp.moveaxis(blocks, 0, dim)
+    shape = blocks.shape
+    return blocks.reshape(*shape[:dim], shape[dim] * shape[dim + 1], *shape[dim + 2 :])
+
+
+def collect(array, axis, dim):
+    size = lax.axis_size(axis)
+    pairs = [(i, (i + 1) % size) for i in range(size)]
+    back = [(b, a) for a, b in pairs]
+    lower, upper = ([], [])
+    for step in range(size - 1):
+        if step % 2 == 0:
+            lower.append(lax.ppermute(lower[-1] if lower else array, axis, pairs))
+        else:
+            upper.append(lax.ppermute(upper[-1] if upper else array, axis, back))
+    parts = jnp.stack([*lower[::-1], array, *upper])
+    shift = lax.axis_index(axis) - len(lower)
+    parts = parts[(jnp.arange(size) - shift) % size]
+    return laid_out(parts, dim)
 
 
 def half_transform(block_data, mu_index, coeff_blocks):
@@ -54,7 +76,7 @@
     half_sums = summed.astype(jnp.bfloat16)
     slab_sums = lax.all_to_all(half_sums, "occ", split_axis=3, concat_axis=2, tiled=True)
     aux_count, slab_rows = (slab_sums.shape[2], slab_sums.shape[3])
-    shard_piece = lax.all_gather(slab_sums, "pair", axis=0, tiled=True)
+    shard_piece = collect(slab_sums, "pair", 0)
     piece_blocks = shard_piece.shape[0]
     flat_piece = shard_piece.reshape(piece_blocks * block_width, aux_count, slab_rows)
     result = jnp.einsum("nqi,na->iqa", flat_piece, virt_coeffs, preferred_element_type=jnp.float32)

time: 338 us -> 425 us (1.26)
  starting transfers between devices: 14.2 us -> 91.6 us
  local copies, waits for them, and re-layouts: 70 us -> 100 us
  between operations: 13.5 us -> 0.21 us
  waiting for transfers between devices: 204 us -> 196 us
    all_gather x1 -> x0, waiting for transfers between devices: 174 us -> none  [on_device(): shard_piece = lax.all_gather(slab_sums, 'pair', axis=0, tiled=True)]
    ppermute x0 -> x7, waiting for transfers between devices: none -> 167 us  [the longest x4 167 us: collect(): lower.append(lax.ppermute(lower[-1] if lower else array, axis, pairs))]
    ppermute x0 -> x7, starting transfers between devices: none -> 77.4 us  [the longest x3 71 us: collect(): upper.append(lax.ppermute(upper[-1] if upper else array, axis, back))]
    gather x0 -> x2, local copies, waits for them, and re-layouts: none -> 24.8 us  [collect(): parts = parts[(jnp.arange(size) - shift) % size]]
    another operation x0 -> x2, local copies, waits for them, and re-layouts: none -> 22.8 us  [the longest x1 21.3 us: on_device(): shard_piece.reshape(piece_blocks * block_width, aux_count, slab_rows)]
    reshape x1 -> x0, local copies, waits for them, and re-layouts: 16.9 us -> none  [on_device(): shard_piece.reshape(piece_blocks * block_width, aux_count, slab_rows)]
    unnamed x7 -> x24, local copies, waits for them, and re-layouts: 4.67 us -> 20.7 us
    all_gather x1 -> x0, local copies, waits for them, and re-layouts: 14.5 us -> none  [on_device(): shard_piece = lax.all_gather(slab_sums, 'pair', axis=0, tiled=True)]
  transfers between devices with their start and end apart: 4 -> 10, of which waited for: 4 -> 7; matrix products, arithmetic and copies ran while one was open for 2% -> 5% of each run, Pallas kernels for 0% -> 0%
where the time goes in v1:
time: 425 us; the launch traced here: 424 us
  waiting for transfers between devices  196 us (46%)
  local copies, waits for them, and re-layouts  100 us (24%)
  starting transfers between devices  91.6 us (22%)
  matrix products  17.3 us (4%)
  blocking collectives  14.7 us (3%)
    ppermute x4, waiting for transfers between devices, collect(): lower.append(lax.ppermute(lower[-1] if lower else array, axis, pairs))  167 us
    ppermute x3, starting transfers between devices, collect(): upper.append(lax.ppermute(upper[-1] if upper else array, axis, back))  71 us
    gather x2, local copies, waits for them, and re-layouts, collect(): parts = parts[(jnp.arange(size) - shift) % size]  24.8 us
    another operation x1, local copies, waits for them, and re-layouts, on_device(): shard_piece.reshape(piece_blocks * block_width, aux_count, slab_rows)  21.3 us
    unnamed x24, local copies, waits for them, and re-layouts  20.7 us
    all_to_all x1, waiting for transfers between devices, on_device(): lax.all_to_all(send_blocks, 'pair', split_axis=0, concat_axis=0, tiled=True)  19.8 us
    all_to_all x1, blocking collectives, on_device(): lax.all_to_all(half_sums, 'occ', split_axis=3, concat_axis=2, tiled=True)  14.7 us
    dot_general x1, matrix products, on_device(): jnp.einsum('nqi,na->iqa', flat_piece, virt_coeffs, preferred_element_type...  9.58 us
  transfers between devices with their start and end apart: 10, of which 7 were waited for; matrix products, arithmetic and copies ran while one was open for 5% of the time, Pallas kernels for 0%

profile of v1, /device:TPU:0, one launch (start us, length us, event | category | flops | bytes accessed | tf_op | source)
XLA Modules:
  0.0 423.7 jit_solution(5287285329561189950)
XLA Ops:
  5.3 7.3 %all-to-all-start.2 = ((s32[8,1,4]{2,1,0:T(1,128)}), s32[8,1,4]{2,1,0:T(1,128)S(1)}, u32[]{:S(2)}, u32[]{:S(2)}) async-start(s32[8,1,4]{2,1,0:T(1,128)} %bitcast.9), calls=%async_computation.2 | async-start | bytes 8192 | tf_op jit(solution)/shard_map/all_to_all | solution.py:63
  14.7 4.3 %all-to-all-done.2 = s32[8,1,4]{2,1,0:T(1,128)S(1)} async-done(((s32[8,1,4]{2,1,0:T(1,128)}), s32[8,1,4]{2,1,0:T(1,128)S(1)}, u32[]{:S(2)}, u32[]{:S(2)}) %all-to-all-start.2) | async-done | bytes 160 | tf_op jit(solution)/shard_map/all_to_all | solution.py:63
  19.0 3.3 all-to-all-start
  23.5 5.3 %all-to-all-done = s32[8,1,4]{2,1,0:T(1,128)S(1)} async-done(((s32[8,1,4]{2,1,0:T(1,128)}), s32[8,1,4]{2,1,0:T(1,128)S(1)}, u32[]{:S(2)}, u32[]{:S(2)}) %all-to-all-start) | async-done | bytes 160 | tf_op jit(solution)/shard_map/all_to_all | solution.py:64
  28.8 3.6 all-to-all-start.1
  36.1 19.8 %all-to-all-done.1 = bf16[8,4,64,256]{3,2,1,0:T(8,128)(2,1)S(1)} async-done(((bf16[8,4,64,256]{3,2,1,0:T(8,128)(2,1)}), bf16[8,4,64,256]{3,2,1,0:T(8,128)(2,1)S(1)}, u32[]{:S(2)}, u32[]{:S(2)}) %all-to-all-start.1) | async-done | bytes 1048608 | tf_op jit(solution)/shard_map/all_to_all | solution.py:62
  58.6 5.6 %copy.46 = f32[32,64,4,128]{3,2,1,0:T(4,128)} copy(f32[32,64,4,128]{3,1,2,0:T(8,128)S(1)} %fusion.4) | data formatting | bytes 8388608 | tf_op jit(solution)/shard_map/snqm,smi->snqi/dot_general | solution.py:36
  64.2 5.7 %reshape.193 = f32[32,32768]{1,0:T(8,128)} reshape(f32[32,64,4,128]{3,2,1,0:T(4,128)} %copy.46) | data formatting | bytes 8388608 | tf_op jit(solution)/shard_map/reshape | solution.py:72
  69.8 6.1 %dot_general.15 = f32[64,4,128,32]{2,1,0,3:T(4,128)} reshape(f32[32768,32]{0,1:T(8,128)} %bitcast.69) | data formatting | bytes 8388608 | tf_op jit(solution)/shard_map/dot_general | solution.py:70
  75.9 5.9 %fusion.6 = bf16[12,64,4,128]{3,0,2,1:T(8,128)(2,1)S(1)} fusion(f32[64,4,128,32]{2,1,0,3:T(4,128)} %dot_general.15, s32[32]{0:T(128)S(1)} %and_select_fusion.1), kind=kOutput, calls=%fused_computation.19 | convolution fusion | flops 151388544 | bytes 4980864 | tf_op jit(solution)/shard_map/dot_general | solution.py:70
  81.8 4.1 copy.48
  87.4 14.7 %all_to_all.41 = bf16[4,2,49152]{2,1,0:T(2,128)(2,1)} all-to-all(bf16[4,2,49152]{2,1,0:T(2,128)(2,1)S(1)} %reshape.272), channel_id=1, replica_groups=mesh['pair'=8,'occ'=4] {'occ'}, dimensions={0} | all-to-all | bytes 1572864 | tf_op jit(solution)/shard_map/all_to_all | solution.py:77
  107.0 37.2 %collective-permute-done = bf16[12,64,16,32]{1,3,2,0:T(8,128)(2,1)S(1)} collective-permute-done((bf16[12,64,16,32]{1,3,2,0:T(8,128)(2,1)S(1)}, bf16[12,64,16,32]{1,3,2,0:T(8,128)(2,1)S(1)}, u32[]{:S(2)}, u32[]{:S(2)}) %collective-permute-start) | collective-permute-done | bytes 786464 | tf_op jit(solution)/shard_map/ppermute | solution.py:22
  144.3 4.7 %collective-permute-start.4 = (bf16[12,64,16,32]{1,3,2,0:T(8,128)(2,1)S(1)}, bf16[12,64,16,32]{1,3,2,0:T(8,128)(2,1)}, u32[]{:S(2)}, u32[]{:S(2)}) collective-permute-start(bf16[12,64,16,32]{1,3,2,0:T(8,128)(2,1)S(1)} %bitcast.71), channel_id=1, source_target_pairs={{4,0},{8,4},{12,8},{16,12},{20,16},{24,20},{28,24},{0,28},{5,1},{9... | collective-permute-start | bytes 2359304 | tf_op jit(solution)/shard_map/ppermute | solution.py:24
  149.0 61.7 %collective-permute-done.1 = bf16[12,64,16,32]{1,3,2,0:T(8,128)(2,1)S(1)} collective-permute-done((bf16[12,64,16,32]{1,3,2,0:T(8,128)(2,1)S(1)}, bf16[12,64,16,32]{1,3,2,0:T(8,128)(2,1)S(1)}, u32[]{:S(2)}, u32[]{:S(2)}) %collective-permute-start.1) | collective-permute-done | bytes 786464 | tf_op jit(solution)/shard_map/ppermute | solution.py:22
  213.2 32.9 %collective-permute-start.5 = (bf16[12,64,16,32]{1,3,2,0:T(8,128)(2,1)}, bf16[12,64,16,32]{1,3,2,0:T(8,128)(2,1)}, u32[]{:S(2)}, u32[]{:S(2)}) collective-permute-start(bf16[12,64,16,32]{1,3,2,0:T(8,128)(2,1)} %collective-permute-done.4), channel_id=1, source_target_pairs={{4,0},{8,4},{12,8},{16,12},{20,16},{24,20},{28,24},{0,28},{5,1},{9... | collective-permute-start | bytes 2359304 | tf_op jit(solution)/shard_map/ppermute | solution.py:24
  246.0 34.4 %collective-permute-done.2 = bf16[12,64,16,32]{1,3,2,0:T(8,128)(2,1)} collective-permute-done((bf16[12,64,16,32]{1,3,2,0:T(8,128)(2,1)S(1)}, bf16[12,64,16,32]{1,3,2,0:T(8,128)(2,1)}, u32[]{:S(2)}, u32[]{:S(2)}) %collective-permute-start.2) | collective-permute-done | bytes 786464 | tf_op jit(solution)/shard_map/ppermute | solution.py:22
  283.0 33.4 %collective-permute-start.6 = (bf16[12,64,16,32]{1,3,2,0:T(8,128)(2,1)}, bf16[12,64,16,32]{1,3,2,0:T(8,128)(2,1)S(1)}, u32[]{:S(2)}, u32[]{:S(2)}) collective-permute-start(bf16[12,64,16,32]{1,3,2,0:T(8,128)(2,1)} %collective-permute-done.5), channel_id=1, source_target_pairs={{4,0},{8,4},{12,8},{16,12},{20,16},{24,20},{28,24},{0,28},{5,1},{9... | collective-permute-start | bytes 2359304 | tf_op jit(solution)/shard_map/ppermute | solution.py:24
  316.5 33.2 %collective-permute-done.3 = bf16[12,64,16,32]{1,3,2,0:T(8,128)(2,1)} collective-permute-done((bf16[12,64,16,32]{1,3,2,0:T(8,128)(2,1)}, bf16[12,64,16,32]{1,3,2,0:T(8,128)(2,1)}, u32[]{:S(2)}, u32[]{:S(2)}) %collective-permute-start.3) | collective-permute-done | bytes 786464 | tf_op jit(solution)/shard_map/ppermute | solution.py:22
  359.7 2.9 bitcast_dynamic-update-slice_fusion.2
  366.9 11.0 %gather_fusion.4 = bf16[8,12,64,16,32]{2,4,3,1,0:T(8,128)(2,1)} fusion(bf16[8,12,64,16,32]{2,4,3,1,0:T(8,128)(2,1)} %bitcast_dynamic-update-slice_fusion, s32[1024]{0:T(1024)S(1)} %pad_clamp_fusion), kind=kCustom, calls=%fused_computation.4 | custom fusion | bytes 12582944 | tf_op jit(solution)/shard_map/gather | solution.py:27
  377.9 13.8 %copy.52 = bf16[8,12,64,16,32]{2,1,0,4,3:T(8,128)(2,1)} copy(bf16[8,12,64,16,32]{2,4,3,1,0:T(8,128)(2,1)} %gather_fusion.4) | data formatting | bytes 12582912 | tf_op jit(solution)/shard_map/gather | solution.py:27
  391.7 21.3 %reshape_reshape.7 = bf16[6144,16,32]{0,2,1:T(8,128)(2,1)} reshape(bf16[8,12,64,16,32]{2,1,0,4,3:T(8,128)(2,1)} %copy.52) | data formatting | bytes 12582912 | tf_op jit(solution)/shard_map/reshape;reshape | solution.py:81
  413.1 9.6 %fusion.12 = bf16[32,16,640]{2,0,1:T(8,128)(2,1)S(1)} fusion(bf16[6144,16,32]{0,2,1:T(8,128)(2,1)} %reshape_reshape.7, bf16[6144,640]{1,0:T(8,128)(2,1)} %param.7), kind=kOutput, calls=%fused_computation.21 | convolution fusion | flops 4026859520 | bytes 14811136 | tf_op jit(solution)/shard_map/nqi,na->iqa/dot_general | solution.py:82
  (74 shorter events, 41.8 us)
Async XLA Ops:
  0.0 12.6 %copy-start = (bf16[1,64,64,256]{3,2,1,0:T(8,128)(2,1)S(1)}, bf16[1,64,64,256]{3,2,1,0:T(8,128)(2,1)}, u32[]{:S(2)}) copy-start(bf16[1,64,64,256]{3,2,1,0:T(8,128)(2,1)} %param.5) | copy-start | bytes 6291460
  0.0 3.9 copy-start.6
  5.3 13.7 %all-to-all-start.2 = ((s32[8,1,4]{2,1,0:T(1,128)}), s32[8,1,4]{2,1,0:T(1,128)S(1)}, u32[]{:S(2)}, u32[]{:S(2)}) async-start(s32[8,1,4]{2,1,0:T(1,128)} %bitcast.9), calls=%async_computation.2 | async-start | bytes 8192 | tf_op jit(solution)/shard_map/all_to_all | solution.py:63
  19.0 9.8 %all-to-all-start = ((s32[8,1,4]{2,1,0:T(1,128)}), s32[8,1,4]{2,1,0:T(1,128)S(1)}, u32[]{:S(2)}, u32[]{:S(2)}) async-start(s32[8,1,4]{2,1,0:T(1,128)} %bitcast.2), calls=%async_computation | async-start | bytes 8192 | tf_op jit(solution)/shard_map/all_to_all | solution.py:64
  28.8 27.1 %all-to-all-start.1 = ((bf16[8,4,64,256]{3,2,1,0:T(8,128)(2,1)}), bf16[8,4,64,256]{3,2,1,0:T(8,128)(2,1)S(1)}, u32[]{:S(2)}, u32[]{:S(2)}) async-start(bf16[8,4,64,256]{3,2,1,0:T(8,128)(2,1)} %broadcast_multiply_fusion), calls=%async_computation.1 | async-start | bytes 2097152 | tf_op jit(solution)/shard_map/all_to_all | solution.py:62
  105.7 38.5 %collective-permute-start = (bf16[12,64,16,32]{1,3,2,0:T(8,128)(2,1)S(1)}, bf16[12,64,16,32]{1,3,2,0:T(8,128)(2,1)S(1)}, u32[]{:S(2)}, u32[]{:S(2)}) collective-permute-start(bf16[12,64,16,32]{1,3,2,0:T(8,128)(2,1)S(1)} %bitcast.70), channel_id=1, source_target_pairs={{0,4},{4,8},{8,12},{12,16},{16,20},{20,24},{24,28},{28,0},{1,5},{5... | collective-permute-start | bytes 2359304 | tf_op jit(solution)/shard_map/ppermute | solution.py:22
  144.3 68.9 %copy-start.2 = (bf16[12,64,16,32]{1,3,2,0:T(8,128)(2,1)}, bf16[12,64,16,32]{1,3,2,0:T(8,128)(2,1)S(1)}, u32[]{:S(2)}) copy-start(bf16[12,64,16,32]{1,3,2,0:T(8,128)(2,1)S(1)} %collective-permute-done) | copy-start | bytes 2359300
  144.3 66.4 %collective-permute-start.1 = (bf16[12,64,16,32]{1,3,2,0:T(8,128)(2,1)S(1)}, bf16[12,64,16,32]{1,3,2,0:T(8,128)(2,1)S(1)}, u32[]{:S(2)}, u32[]{:S(2)}) collective-permute-start(bf16[12,64,16,32]{1,3,2,0:T(8,128)(2,1)S(1)} %collective-permute-done), channel_id=1, source_target_pairs={{0,4},{4,8},{8,12},{12,16},{16,20},{20,24},{24,28},{28,0},{1,5},{5... | collective-permute-start | bytes 2359304 | tf_op jit(solution)/shard_map/ppermute | solution.py:22
  144.3 68.9 %collective-permute-start.4 = (bf16[12,64,16,32]{1,3,2,0:T(8,128)(2,1)S(1)}, bf16[12,64,16,32]{1,3,2,0:T(8,128)(2,1)}, u32[]{:S(2)}, u32[]{:S(2)}) collective-permute-start(bf16[12,64,16,32]{1,3,2,0:T(8,128)(2,1)S(1)} %bitcast.71), channel_id=1, source_target_pairs={{4,0},{8,4},{12,8},{16,12},{20,16},{24,20},{28,24},{0,28},{5,1},{9... | collective-permute-start | bytes 2359304 | tf_op jit(solution)/shard_map/ppermute | solution.py:24
  210.7 35.4 %copy-start.4 = (bf16[12,64,16,32]{1,3,2,0:T(8,128)(2,1)}, bf16[12,64,16,32]{1,3,2,0:T(8,128)(2,1)S(1)}, u32[]{:S(2)}) copy-start(bf16[12,64,16,32]{1,3,2,0:T(8,128)(2,1)S(1)} %collective-permute-done.1) | copy-start | bytes 2359300
  210.7 69.7 %collective-permute-start.2 = (bf16[12,64,16,32]{1,3,2,0:T(8,128)(2,1)S(1)}, bf16[12,64,16,32]{1,3,2,0:T(8,128)(2,1)}, u32[]{:S(2)}, u32[]{:S(2)}) collective-permute-start(bf16[12,64,16,32]{1,3,2,0:T(8,128)(2,1)S(1)} %collective-permute-done.1), channel_id=1, source_target_pairs={{0,4},{4,8},{8,12},{12,16},{16,20},{20,24},{24,28},{28,0},{1,5},{5... | collective-permute-start | bytes 2359304 | tf_op jit(solution)/shard_map/ppermute | solution.py:22
  213.2 69.9 %collective-permute-start.5 = (bf16[12,64,16,32]{1,3,2,0:T(8,128)(2,1)}, bf16[12,64,16,32]{1,3,2,0:T(8,128)(2,1)}, u32[]{:S(2)}, u32[]{:S(2)}) collective-permute-start(bf16[12,64,16,32]{1,3,2,0:T(8,128)(2,1)} %collective-permute-done.4), channel_id=1, source_target_pairs={{4,0},{8,4},{12,8},{16,12},{20,16},{24,20},{28,24},{0,28},{5,1},{9... | collective-permute-start | bytes 2359304 | tf_op jit(solution)/shard_map/ppermute | solution.py:24
  280.4 69.3 %collective-permute-start.3 = (bf16[12,64,16,32]{1,3,2,0:T(8,128)(2,1)}, bf16[12,64,16,32]{1,3,2,0:T(8,128)(2,1)}, u32[]{:S(2)}, u32[]{:S(2)}) collective-permute-start(bf16[12,64,16,32]{1,3,2,0:T(8,128)(2,1)} %collective-permute-done.2), channel_id=1, source_target_pairs={{0,4},{4,8},{8,12},{12,16},{16,20},{20,24},{24,28},{28,0},{1,5},{5... | collective-permute-start | bytes 2359304 | tf_op jit(solution)/shard_map/ppermute | solution.py:22
  283.0 72.4 %copy-start.5 = (bf16[12,64,16,32]{1,3,2,0:T(8,128)(2,1)S(1)}, bf16[12,64,16,32]{1,3,2,0:T(8,128)(2,1)}, u32[]{:S(2)}) copy-start(bf16[12,64,16,32]{1,3,2,0:T(8,128)(2,1)} %copy-done.4) | copy-start | bytes 2359300
  283.0 73.8 %copy-start.3 = (bf16[12,64,16,32]{1,3,2,0:T(8,128)(2,1)S(1)}, bf16[12,64,16,32]{1,3,2,0:T(8,128)(2,1)}, u32[]{:S(2)}) copy-start(bf16[12,64,16,32]{1,3,2,0:T(8,128)(2,1)} %copy-done.2) | copy-start | bytes 2359300
  283.0 82.5 %collective-permute-start.6 = (bf16[12,64,16,32]{1,3,2,0:T(8,128)(2,1)}, bf16[12,64,16,32]{1,3,2,0:T(8,128)(2,1)S(1)}, u32[]{:S(2)}, u32[]{:S(2)}) collective-permute-start(bf16[12,64,16,32]{1,3,2,0:T(8,128)(2,1)} %collective-permute-done.5), channel_id=1, source_target_pairs={{4,0},{8,4},{12,8},{16,12},{20,16},{24,20},{28,24},{0,28},{5,1},{9... | collective-permute-start | bytes 2359304 | tf_op jit(solution)/shard_map/ppermute | solution.py:24
  413.1 10.6 %copy-start.1 = (bf16[1,64,64,256]{3,2,1,0:T(8,128)(2,1)S(1)}, bf16[1,64,64,256]{3,2,1,0:T(8,128)(2,1)}, u32[]{:S(2)}) copy-start(bf16[1,64,64,256]{3,2,1,0:T(8,128)(2,1)} %param.5) | copy-start | bytes 6291460
